TPU v7x, 32 devices: a whole 2x2x4 slice. The times are simulated.
32 devices in a mesh: grid: 4 (over z), elec: 8 (over y, x, core).
Axes of the slice: x: 2, y: 2, z: 4, core: 2. Of those that a mesh axis runs over, the one named last changes fastest.
Arguments:
- electric: bfloat16 [2, 8192, 8192], P(None, 'elec', 'grid'), may hold values from -6 to 6
- trial: bfloat16 [8192, 2, 128], P('grid'), may hold values from -0.0625 to 0.0625
- counts: int32 [8], replicated, may hold values from 1 to 1024, as said below
Outputs:
- field: float32 [8192, 2, 128], P(('grid', 'elec'))
Inputs may be any that keep to these rules, and one draw needn't show every extreme that they name: `counts`: at least one group holds exactly 1024 live electrons.
All inputs are finite; a program needn't handle non-finite values.
Results may differ from a plain program's by a relative error of at most 0.0023.
Values sent between devices are 32-bit elements; how exact they have to be, the bound alone decides.
A program may use at most 64 MiB of HBM per device.

v0:
```python
import jax
import jax.numpy as jnp
from jax import lax
from jax.sharding import PartitionSpec as P


def margin_block(electric_slab, trial_flat, mode_count):
    slab_count = electric_slab.shape[1]
    flattened = electric_slab.reshape(2 * slab_count, electric_slab.shape[2])
    products = jnp.dot(flattened, trial_flat, preferred_element_type=jnp.float32)
    real_part = products[:slab_count, :mode_count] + products[slab_count:, mode_count:]
    imag_part = products[:slab_count, mode_count:] - products[slab_count:, :mode_count]
    return jnp.stack([real_part, imag_part])


def field_block(electric_slab, coef_real, coef_imag):
    slab_count = electric_slab.shape[1]
    flattened = electric_slab.reshape(2 * slab_count, electric_slab.shape[2])
    coef_matrix = jnp.concatenate(
        [jnp.concatenate([coef_real, coef_imag], 1), jnp.concatenate([-coef_imag, coef_real], 1)], 0
    )
    return lax.dot_general(
        flattened, coef_matrix, (((0,), (0,)), ((), ())), preferred_element_type=jnp.float32
    )


def body(electric, trial, counts):
    capacity = electric.shape[1]
    points = electric.shape[2]
    mode_count = trial.shape[2]
    trial_flat = trial.reshape(points, 2 * mode_count)
    group_index = lax.axis_index("elec")
    live_count = lax.dynamic_slice_in_dim(counts, group_index, 1, 0)[0]
    total_live = jnp.sum(counts.astype(jnp.float32))
    partial_margins = margin_block(electric, trial_flat, mode_count)
    margins = lax.psum(partial_margins, "grid")
    slot_ids = jnp.arange(capacity, dtype=jnp.int32)
    weights = jnp.where(slot_ids < live_count, 1.0, 0.0).astype(jnp.float32) * (
        1.0 / jnp.sqrt(total_live)
    )
    coefs = (margins * weights[None, :, None]).astype(jnp.bfloat16)
    coef_real = coefs[0]
    coef_imag = coefs[1]
    share = points // lax.axis_size("elec")
    mine = lax.psum_scatter(
        field_block(electric, coef_real, coef_imag), "elec", scatter_dimension=0, tiled=True
    )
    return mine.reshape(share, 2, mode_count)


def solution(mesh):
    placed = (P(None, "elec", "grid"), P("grid", None, None), P())
    return jax.shard_map(
        body, mesh=mesh, in_specs=placed, out_specs=P(("grid", "elec"), None, None), check_vma=False
    )
```

profile of v0, /device:TPU:0, one launch (start us, length us, event | category | flops | bytes accessed | tf_op | source)
XLA Modules:
  0.0 126.5 jit_solution(7639683581927419735)
XLA Ops:
  6.5 0.0 all-reduce.2.cloned.1.call-start
  6.5 6.1 %fusion = f32[2048,256]{1,0:T(8,128)S(1)} fusion(bf16[2048,2048]{1,0:T(8,128)(2,1)} %bitcast.22, bf16[256,8,2,128]{3,2,1,0:T(2,128)(2,1)} %bitcast.24), kind=kOutput, calls=%fused_computation.1 | convolution fusion | flops 2147483648 | bytes 11534336 | tf_op jit(solution)/shard_map/dot_general | solution.py:10
  12.6 0.1 fusion.11
  12.7 0.0 copy-start
  12.7 1.1 pad_maximum_fusion
  13.8 0.0 all-reduce.2.cloned.1.call-update
  13.9 0.0 reduce-scatter.2.cloned.1.call-start
  13.9 0.0 copy-done
  13.9 0.6 convert_reduce_fusion
  15.2 0.6 dynamic_slice.3
  15.8 0.6 select_multiply_fusion
  16.5 52.2 %all-reduce.2.cloned.1.call-done = f32[2,1024,128]{2,1,0:T(8,128)} async-done(((f32[2,1024,128]{2,1,0:T(8,128)}), f32[2,1024,128]{2,1,0:T(8,128)}) %all-reduce.2.cloned.1.call-update) | async-done | bytes 1048592 | tf_op jit(solution)/shard_map/psum | solution.py:36
  68.7 1.4 %multiply_convert_fusion = bf16[2,1024,128]{2,1,0:T(8,128)(2,1)S(1)} fusion(f32[2,1024,128]{2,1,0:T(8,128)} %all-reduce.2.cloned.1.call-done, f32[1024]{0:T(1024)S(1)} %select_multiply_fusion), kind=kLoop, calls=%fused_computation.12 | loop fusion | flops 524288 | bytes 1576960 | tf_op jit(solution)/shard_map/convert_element_type | solution.py:41
  70.2 7.1 %convolution_bitcast_fusion = f32[2048,256]{0,1:T(8,128)} fusion(bf16[2048,2048]{1,0:T(8,128)(2,1)} %bitcast.23, bf16[1024,128]{1,0:T(8,128)(2,1)S(1)} %get-tuple-element.8, bf16[1024,128]{1,0:T(8,128)(2,1)S(1)} %fusion.13, bf16[1024,128]{1,0:T(8,128)(2,1)S(1)} %get-tuple-element.7), kind=kOutput, calls=%fused_computation | convolution fusion | flops 2151677952 | bytes 11272192 | tf_op jit(solution)/shard_map/dot_general | solution.py:22
  77.3 0.0 reduce-scatter.2.cloned.1.call-update
  77.3 40.5 %reduce-scatter.2.cloned.1.call-done = f32[256,256]{0,1:T(8,128)} async-done(((f32[2048,256]{0,1:T(8,128)}), f32[256,256]{0,1:T(8,128)}) %reduce-scatter.2.cloned.1.call-update) | async-done | bytes 262160 | tf_op jit(solution)/shard_map/reduce_scatter | solution.py:45
  117.8 1.8 %copy.4 = f32[256,2,128]{2,1,0:T(2,128)} copy(f32[256,2,128]{0,2,1:T(8,128)} %bitcast.21) | data formatting | bytes 524288 | tf_op jit(solution)/shard_map/reshape | solution.py:48
  (2 shorter events, 0.1 us)
Async XLA Ops:
  6.5 62.1 %all-reduce.2.cloned.1.call-start = ((), (), s32[]{:S(2)}) async-start(), calls=%async_computation.1 | async-start | bytes 2097152 | tf_op jit(solution)/shard_map/psum | solution.py:36
  12.7 1.2 copy-start
  13.9 104.0 %reduce-scatter.2.cloned.1.call-start = ((), (), s32[]{:S(2)}) async-start(), calls=%async_computation.2 | async-start | bytes 2359296 | tf_op jit(solution)/shard_map/reduce_scatter | solution.py:45
Sparse Core Ops, SparseCore 0:
  14.0 54.6 all-reduce.1
  77.4 40.3 reduce-scatter.1
where the time goes:
time: 127 us; the launch traced here: 126 us
  waiting for transfers between devices  92.7 us (73%)
  between operations  14.2 us (11%)
  matrix products  13.2 us (10%)
  other arithmetic  3.91 us (3%)
  local copies, waits for them, and re-layouts  2.41 us (2%)
    psum x1, waiting for transfers between devices, body(): margins = lax.psum(partial_margins, 'grid')  52.2 us
    reduce_scatter x1, waiting for transfers between devices, body(): lax.psum_scatter(field_block(electric, coef_real, coef_imag), 'elec', sca...  40.5 us
    dot_general x1, matrix products, field_block(): lax.dot_general(flattened, coef_matrix, (((0,), (0,)), ((), ())), preferr...  7.11 us
    dot_general x1, matrix products, margin_block(): jnp.dot(flattened, trial_flat, preferred_element_type=jnp.float32)  6.08 us
  transfers between devices with their start and end apart: 2, of which 2 were waited for; matrix products, arithmetic and copies ran while one was open for 1% of the time, Pallas kernels for 0%

commit v1 on v0

v1 whole, which is shorter than its diff:
```python
import functools

import jax
import jax.numpy as jnp
from jax import lax
from jax.experimental import pallas as pl
from jax.experimental.pallas import tpu as pltpu
from jax.sharding import PartitionSpec as P

MESH = pl.DeviceIdType.MESH
HOP = 2


def kernel(
    n, chips, chunks, blocks,
    counts_ref, trial_ref, electric_ref, out_ref,
    ebuf, part, rl, rr, sl, sr, x0, x1, f, r1, g, r2, fin,
    esem, slsem, rlsem, srsem, rrsem, s1s, s1r, s2s, s2r,
):
    cap = ebuf.shape[1]
    points = ebuf.shape[2]
    modes = trial_ref.shape[1]
    mc = modes // chunks
    sl_n = cap // blocks
    pieces = chunks * blocks
    share = f.shape[-1]
    i = lax.axis_index("grid")
    e = lax.axis_index("elec")
    core = lax.rem(e, 2)
    chip = lax.div(e, 2)
    partner = e + 1 - 2 * core

    def load(s, z):
        return pltpu.make_async_copy(
            electric_ref.at[z, pl.ds(s * sl_n, sl_n), :],
            ebuf.at[z, pl.ds(s * sl_n, sl_n), :],
            esem.at[s, z],
        )

    for s in range(blocks):
        load(s, 0).start()
        load(s, 1).start()

    barrier = pltpu.get_barrier_semaphore()

    for d in (1, n - 1):
        pl.semaphore_signal(barrier, inc=1, device_id=(lax.rem(i + d, n), e), device_id_type=MESH)

    pl.semaphore_signal(barrier, inc=1, device_id=(i, partner), device_id_type=MESH)
    for d in range(1, chips):
        q = lax.rem(chip + d, chips)
        pl.semaphore_signal(barrier, inc=1, device_id=(i, 2 * q + core), device_id_type=MESH)

    def right(k, src):
        return pltpu.make_async_remote_copy(
            src_ref=src.at[k], dst_ref=rl.at[k], send_sem=slsem.at[k], recv_sem=rlsem.at[k],
            device_id=(i + 1, e), device_id_type=MESH,
        )

    def left(k, src):
        return pltpu.make_async_remote_copy(
            src_ref=src.at[k], dst_ref=rr.at[k], send_sem=srsem.at[k], recv_sem=rrsem.at[k],
            device_id=(i - 1, e), device_id_type=MESH,
        )

    def send_ends(k):
        @pl.when(i == 0)
        def _():
            right(k, part).start()

        @pl.when(i == n - 1)
        def _():
            left(k, part).start()

    vt = trial_ref[...].reshape(2 * modes, points)
    dims = (((1,), (1,)), ((), ()))
    for s in range(blocks):
        load(s, 0).wait()
        load(s, 1).wait()
        q0 = lax.dot_general(vt, ebuf[0, s * sl_n:(s + 1) * sl_n, :], dims, preferred_element_type=jnp.float32)
        q1 = lax.dot_general(vt, ebuf[1, s * sl_n:(s + 1) * sl_n, :], dims, preferred_element_type=jnp.float32)
        real = q0[:modes] + q1[modes:]
        imag = q0[modes:] - q1[:modes]
        for c in range(chunks):
            part[c * blocks + s, :mc] = real[c * mc:(c + 1) * mc]
            part[c * blocks + s, mc:] = imag[c * mc:(c + 1) * mc]
        if s == 0:
            pl.semaphore_wait(barrier, chips + 2)
        send_ends(s)

    def rest(k, _):
        send_ends(k)
        return 0

    lax.fori_loop(blocks, pieces, rest, 0)

    live = counts_ref[e]
    total_live = lax.fori_loop(0, 2 * chips, lambda j, v: v + counts_ref[j], jnp.int32(0))
    scaling = 1.0 / jnp.sqrt(jnp.full((8, sl_n), total_live, jnp.int32).astype(jnp.float32))
    scaling = scaling[:1]

    def exchange(c):
        return pltpu.make_async_remote_copy(
            src_ref=f.at[c, 1 - core], dst_ref=r1.at[c], send_sem=s1s.at[c], recv_sem=s1r.at[c],
            device_id=(i, partner), device_id_type=MESH,
        )

    def scatter(c, q, slot):
        return pltpu.make_async_remote_copy(
            src_ref=g.at[c, q], dst_ref=r2.at[c, slot], send_sem=s2s.at[c, q], recv_sem=s2r.at[c, slot],
            device_id=(i, 2 * q + core), device_id_type=MESH,
        )

    def step(t, _):
        kl = t - i * HOP
        kr = t - (n - 1 - i) * HOP
        kt = t - (n - 1) * HOP

        @pl.when((i > 0) & (kl >= 0) & (kl < pieces))
        def _():
            right(kl, sl).wait_recv()

            @pl.when(i < n - 1)
            def _():
                sl[kl] = rl[kl] + part[kl]
                right(kl, sl).start()

        @pl.when((i < n - 1) & (kr >= 0) & (kr < pieces))
        def _():
            left(kr, sr).wait_recv()

            @pl.when(i > 0)
            def _():
                sr[kr] = rr[kr] + part[kr]
                left(kr, sr).start()

        @pl.when((kt >= 0) & (kt < pieces))
        def _():
            c = lax.div(kt, blocks)
            s = lax.rem(kt, blocks)
            at = pl.ds(pl.multiple_of(s * sl_n, sl_n), sl_n)

            def finish(total):
                ids = s * sl_n + lax.broadcasted_iota(jnp.int32, (1, sl_n), 1)
                weight = jnp.where(ids < live, 1.0, 0.0).astype(jnp.float32) * scaling
                coef = (total * weight).astype(jnp.bfloat16)
                x0[c, :, at] = coef
                x1[c, :mc, at] = -coef[mc:]
                x1[c, mc:, at] = coef[:mc]

            @pl.when(i == 0)
            def _():
                finish(part[kt] + rr[kt])

            @pl.when(i == n - 1)
            def _():
                finish(part[kt] + rl[kt])

            @pl.when((i > 0) & (i < n - 1))
            def _():
                finish(part[kt] + rl[kt] + rr[kt])

            @pl.when(s == blocks - 1)
            def _():
                width = 256 if points % 256 == 0 else share
                for b in range(points // width):
                    cols = slice(b * width, (b + 1) * width)
                    acc = jnp.dot(x0[c], ebuf[0, :, cols], preferred_element_type=jnp.float32)
                    acc += jnp.dot(x1[c], ebuf[1, :, cols], preferred_element_type=jnp.float32)
                    for j in range(width // share):
                        owner = b * (width // share) + j
                        f[c, owner % 2, owner // 2] = acc[:, j * share:(j + 1) * share]
                exchange(c).start()

        kx = kt - 2

        @pl.when((kx >= 0) & (kx < pieces) & (lax.rem(kx, blocks) == blocks - 1))
        def _():
            c = lax.div(kx, blocks)
            exchange(c).wait_recv()
            for d in range(1, chips + 1):
                q = lax.rem(chip + d, chips)
                g[c, q] = f[c, core, q] + r1[c, q]
                if d < chips:
                    scatter(c, q, chip).start()
        return 0

    lax.fori_loop(0, pieces + (n - 1) * HOP + 2, step, 0)

    for c in range(chunks):
        total = g[c, chip]
        for d in range(1, chips):
            q = lax.rem(chip + d, chips)
            scatter(c, q, q).wait_recv()
            total += r2[c, q]
        fin[c * mc:(c + 1) * mc] = total[:mc]
        fin[modes + c * mc:modes + (c + 1) * mc] = total[mc:]
    out_ref[...] = fin[...].T

    def drain(k, _):
        @pl.when(i < n - 1)
        def _():
            right(k, part).wait_send()

        @pl.when(i > 0)
        def _():
            left(k, part).wait_send()
        return 0

    lax.fori_loop(0, pieces, drain, 0)
    for c in range(chunks):
        exchange(c).wait_send()
        for d in range(1, chips):
            q = lax.rem(chip + d, chips)
            scatter(c, q, chip).wait_send()


def body(n, electric, trial, counts):
    cap, points = electric.shape[1:]
    modes = trial.shape[2]
    chips = counts.shape[0] // 2
    share = points // counts.shape[0]
    chunks = 4
    blocks = 4
    pieces = chunks * blocks
    rows = 2 * modes // chunks
    piece = pltpu.VMEM((pieces, rows, cap // blocks), jnp.float32)
    dma = pltpu.SemaphoreType.DMA
    out = pl.pallas_call(
        functools.partial(kernel, n, chips, chunks, blocks),
        out_shape=jax.ShapeDtypeStruct((share, 2 * modes), jnp.float32),
        in_specs=[
            pl.BlockSpec(memory_space=pltpu.SMEM),
            pl.BlockSpec(memory_space=pltpu.VMEM),
            pl.BlockSpec(memory_space=pl.ANY),
        ],
        out_specs=pl.BlockSpec(memory_space=pltpu.VMEM),
        scratch_shapes=[
            pltpu.VMEM((2, cap, points), jnp.bfloat16),
            piece, piece, piece, piece, piece,
            pltpu.VMEM((chunks, rows, cap), jnp.bfloat16),
            pltpu.VMEM((chunks, rows, cap), jnp.bfloat16),
            pltpu.VMEM((chunks, 2, chips, rows, share), jnp.float32),
            pltpu.VMEM((chunks, chips, rows, share), jnp.float32),
            pltpu.VMEM((chunks, chips, rows, share), jnp.float32),
            pltpu.VMEM((chunks, chips, rows, share), jnp.float32),
            pltpu.VMEM((2 * modes, share), jnp.float32),
            dma((blocks, 2)),
            dma((pieces,)), dma((pieces,)), dma((pieces,)), dma((pieces,)),
            dma((chunks,)), dma((chunks,)),
            dma((chunks, chips)), dma((chunks, chips)),
        ],
        compiler_params=pltpu.CompilerParams(
            collective_id=0, has_side_effects=True, vmem_limit_bytes=60 * 1024 * 1024
        ),
    )(counts, jnp.transpose(trial, (1, 2, 0)), electric)
    return out.reshape(share, 2, modes)


def solution(mesh):
    placed = (P(None, "elec", "grid"), P("grid", None, None), P())
    return jax.shard_map(
        functools.partial(body, mesh.shape["grid"]),
        mesh=mesh, in_specs=placed, out_specs=P(("grid", "elec"), None, None), check_vma=False,
    )
```

time: 127 us -> 55.2 us (0.43)
  waiting for transfers between devices: 92.7 us -> 0 us
  Pallas kernels: 0 us -> 49.2 us
  between operations: 14.2 us -> 0.01 us
  matrix products: 13.2 us -> 0 us
  other arithmetic: 3.91 us -> 0 us
  local copies, waits for them, and re-layouts: 2.41 us -> 5.47 us
    psum x1 -> x0, waiting for transfers between devices: 52.2 us -> none  [body(): margins = lax.psum(partial_margins, 'grid')]
    pallas_call x0 -> x1, Pallas kernels: none -> 49.2 us  [body(): pl.pallas_call(functools.partial(kernel, n, chips, chunks, blocks), out_s...]
    reduce_scatter x1 -> x0, waiting for transfers between devices: 40.5 us -> none  [body(): lax.psum_scatter(field_block(electric, coef_real, coef_imag), 'elec', sca...]
    dot_general x2 -> x0, matrix products: 13.2 us -> none  [the longest x1 7.11 us: field_block(): lax.dot_general(flattened, coef_matrix, (((0,), (0,)), ((), ())), preferr...]
    unnamed x2 -> x1, local copies, waits for them, and re-layouts: 0.01 us -> 3.69 us
    convert_element_type x1 -> x0, other arithmetic: 1.42 us -> none  [body(): coefs = (margins * weights[None, :, None]).astype(jnp.bfloat16)]
  transfers between devices with their start and end apart: 2 -> 0, of which waited for: 2 -> 0; matrix products, arithmetic and copies ran while one was open for 1% -> 0% of each run, Pallas kernels for 0% -> 0%
where the time goes in v1:
time: 55.2 us; the launch traced here: 54.6 us
  Pallas kernels  49.2 us (89%)
  local copies, waits for them, and re-layouts  5.47 us (10%)
    pallas_call x1, Pallas kernels, body(): pl.pallas_call(functools.partial(kernel, n, chips, chunks, blocks), out_s...  49.2 us
    unnamed x1, local copies, waits for them, and re-layouts  3.69 us
    reshape x1, local copies, waits for them, and re-layouts, body(): return out.reshape(share, 2, modes)  1.78 us

profile of v1, /device:TPU:0, one launch (start us, length us, event | category | flops | bytes accessed | tf_op | source)
XLA Modules:
  0.0 54.6 jit_solution(15807491475215955868)
XLA Ops:
  0.0 3.7 %copy.4 = bf16[2048,2,128]{0,2,1:T(8,128)(2,1)} copy(bf16[2048,2,128]{2,1,0:T(2,128)(2,1)} %param.4) | data formatting | bytes 2097152 | tf_op args[1]
  3.7 49.2 %shard_map.37 = f32[256,256]{1,0:T(8,128)} custom-call(s32[8]{0:T(128)} %counts_ref.1, bf16[2,128,2048]{2,1,0:T(8,128)(2,1)} %bitcast.1, bf16[2,1024,2048]{2,1,0:T(8,128)(2,1)} %electric_ref.1), custom_call_target="tpu_custom_call" | custom-call | tf_op jit(solution)/shard_map/pallas_call | solution.py:229
  52.9 1.8 %reshape.3 = f32[256,2,128]{2,1,0:T(2,128)} reshape(f32[256,256]{1,0:T(8,128)} %shard_map.37) | data formatting | bytes 524288 | tf_op jit(solution)/shard_map/reshape | solution.py:257

commit v2 on v1

--- a/solution.py
+++ b/solution.py
@@ -9,17 +9,21 @@
 
 MESH = pl.DeviceIdType.MESH
 HOP = 2
+LAG = 3
+CHUNKS = 4
+BLOCKS = 4
 
 
 def kernel(
     n, chips, chunks, blocks,
     counts_ref, trial_ref, electric_ref, out_ref,
-    ebuf, part, rl, rr, sl, sr, x0, x1, f, r1, g, r2, fin,
+    wide, vt, ebuf, part, rl, rr, sl, sr, x0, x1, f, r1, g, r2, fin,
     esem, slsem, rlsem, srsem, rrsem, s1s, s1r, s2s, s2r,
 ):
     cap = ebuf.shape[1]
     points = ebuf.shape[2]
     modes = trial_ref.shape[1]
+    block_chips = max(1, chips // blocks)
     mc = modes // chunks
     sl_n = cap // blocks
     pieces = chunks * blocks
@@ -72,13 +76,16 @@
         def _():
             left(k, part).start()
 
-    vt = trial_ref[...].reshape(2 * modes, points)
+    wide[...] = trial_ref[...].astype(jnp.float32)
+    vt[:modes] = wide[pl.ds(0, points, stride=2), :].astype(jnp.bfloat16).T
+    vt[modes:] = wide[pl.ds(1, points, stride=2), :].astype(jnp.bfloat16).T
+
     dims = (((1,), (1,)), ((), ()))
     for s in range(blocks):
         load(s, 0).wait()
         load(s, 1).wait()
-        q0 = lax.dot_general(vt, ebuf[0, s * sl_n:(s + 1) * sl_n, :], dims, preferred_element_type=jnp.float32)
-        q1 = lax.dot_general(vt, ebuf[1, s * sl_n:(s + 1) * sl_n, :], dims, preferred_element_type=jnp.float32)
+        q0 = lax.dot_general(vt[...], ebuf[0, s * sl_n:(s + 1) * sl_n, :], dims, preferred_element_type=jnp.float32)
+        q1 = lax.dot_general(vt[...], ebuf[1, s * sl_n:(s + 1) * sl_n, :], dims, preferred_element_type=jnp.float32)
         real = q0[:modes] + q1[modes:]
         imag = q0[modes:] - q1[:modes]
         for c in range(chunks):
@@ -99,9 +106,9 @@
     scaling = 1.0 / jnp.sqrt(jnp.full((8, sl_n), total_live, jnp.int32).astype(jnp.float32))
     scaling = scaling[:1]
 
-    def exchange(c):
-        return pltpu.make_async_remote_copy(
-            src_ref=f.at[c, 1 - core], dst_ref=r1.at[c], send_sem=s1s.at[c], recv_sem=s1r.at[c],
+    def exchange(c, q):
+        return pltpu.make_async_remote_copy(
+            src_ref=f.at[c, 1 - core, q], dst_ref=r1.at[c, q], send_sem=s1s.at[c, q], recv_sem=s1r.at[c, q],
             device_id=(i, partner), device_id_type=MESH,
         )
 
@@ -160,32 +167,38 @@
             def _():
                 finish(part[kt] + rl[kt] + rr[kt])
 
-            @pl.when(s == blocks - 1)
-            def _():
-                width = 256 if points % 256 == 0 else share
-                for b in range(points // width):
-                    cols = slice(b * width, (b + 1) * width)
-                    acc = jnp.dot(x0[c], ebuf[0, :, cols], preferred_element_type=jnp.float32)
-                    acc += jnp.dot(x1[c], ebuf[1, :, cols], preferred_element_type=jnp.float32)
-                    for j in range(width // share):
-                        owner = b * (width // share) + j
-                        f[c, owner % 2, owner // 2] = acc[:, j * share:(j + 1) * share]
-                exchange(c).start()
-
-        kx = kt - 2
-
-        @pl.when((kx >= 0) & (kx < pieces) & (lax.rem(kx, blocks) == blocks - 1))
+        kf = kt - blocks
+        uf = lax.rem(kf, blocks) * block_chips
+
+        @pl.when((kf >= 0) & (kf < pieces) & (uf < chips))
+        def _():
+            c = lax.div(kf, blocks)
+            for j in range(block_chips):
+                q = lax.rem(chip + 1 + uf + j, chips)
+                cols = pl.ds(pl.multiple_of(q * 2 * share, 2 * share), 2 * share)
+                acc = jnp.dot(x0[c], ebuf[0, :, cols], preferred_element_type=jnp.float32)
+                acc += jnp.dot(x1[c], ebuf[1, :, cols], preferred_element_type=jnp.float32)
+                f[c, 0, q] = acc[:, :share]
+                f[c, 1, q] = acc[:, share:]
+                exchange(c, q).start()
+
+        kx = kf - LAG
+        ux = lax.rem(kx, blocks) * block_chips
+
+        @pl.when((kx >= 0) & (kx < pieces) & (ux < chips))
         def _():
             c = lax.div(kx, blocks)
-            exchange(c).wait_recv()
-            for d in range(1, chips + 1):
-                q = lax.rem(chip + d, chips)
+            for j in range(block_chips):
+                q = lax.rem(chip + 1 + ux + j, chips)
+                exchange(c, q).wait_recv()
                 g[c, q] = f[c, core, q] + r1[c, q]
-                if d < chips:
+
+                @pl.when(ux + j < chips - 1)
+                def _():
                     scatter(c, q, chip).start()
         return 0
 
-    lax.fori_loop(0, pieces + (n - 1) * HOP + 2, step, 0)
+    lax.fori_loop(0, pieces + (n - 1) * HOP + blocks + LAG, step, 0)
 
     for c in range(chunks):
         total = g[c, chip]
@@ -195,7 +208,8 @@
             total += r2[c, q]
         fin[c * mc:(c + 1) * mc] = total[:mc]
         fin[modes + c * mc:modes + (c + 1) * mc] = total[mc:]
-    out_ref[...] = fin[...].T
+    out_ref[pl.ds(0, share, stride=2), :] = fin[:modes].T
+    out_ref[pl.ds(1, share, stride=2), :] = fin[modes:].T
 
     def drain(k, _):
         @pl.when(i < n - 1)
@@ -209,9 +223,10 @@
 
     lax.fori_loop(0, pieces, drain, 0)
     for c in range(chunks):
-        exchange(c).wait_send()
+        exchange(c, chip).wait_send()
         for d in range(1, chips):
             q = lax.rem(chip + d, chips)
+            exchange(c, q).wait_send()
             scatter(c, q, chip).wait_send()
 
 
@@ -220,15 +235,15 @@
     modes = trial.shape[2]
     chips = counts.shape[0] // 2
     share = points // counts.shape[0]
-    chunks = 4
-    blocks = 4
+    chunks = CHUNKS
+    blocks = BLOCKS
     pieces = chunks * blocks
     rows = 2 * modes // chunks
     piece = pltpu.VMEM((pieces, rows, cap // blocks), jnp.float32)
     dma = pltpu.SemaphoreType.DMA
     out = pl.pallas_call(
         functools.partial(kernel, n, chips, chunks, blocks),
-        out_shape=jax.ShapeDtypeStruct((share, 2 * modes), jnp.float32),
+        out_shape=jax.ShapeDtypeStruct((2 * share, modes), jnp.float32),
         in_specs=[
             pl.BlockSpec(memory_space=pltpu.SMEM),
             pl.BlockSpec(memory_space=pltpu.VMEM),
@@ -236,6 +251,8 @@
         ],
         out_specs=pl.BlockSpec(memory_space=pltpu.VMEM),
         scratch_shapes=[
+            pltpu.VMEM((2 * points, modes), jnp.float32),
+            pltpu.VMEM((2 * modes, points), jnp.bfloat16),
             pltpu.VMEM((2, cap, points), jnp.bfloat16),
             piece, piece, piece, piece, piece,
             pltpu.VMEM((chunks, rows, cap), jnp.bfloat16),
@@ -247,13 +264,13 @@
             pltpu.VMEM((2 * modes, share), jnp.float32),
             dma((blocks, 2)),
             dma((pieces,)), dma((pieces,)), dma((pieces,)), dma((pieces,)),
-            dma((chunks,)), dma((chunks,)),
+            dma((chunks, chips)), dma((chunks, chips)),
             dma((chunks, chips)), dma((chunks, chips)),
         ],
         compiler_params=pltpu.CompilerParams(
             collective_id=0, has_side_effects=True, vmem_limit_bytes=60 * 1024 * 1024
         ),
-    )(counts, jnp.transpose(trial, (1, 2, 0)), electric)
+    )(counts, trial.reshape(2 * points, modes), electric)
     return out.reshape(share, 2, modes)
 
 

time: 55.2 us -> 52.6 us (0.953)
  local copies, waits for them, and re-layouts: 5.47 us -> 1.67 us
  Pallas kernels: 49.2 us -> 50.7 us
    unnamed x1, local copies, waits for them, and re-layouts: 3.69 us -> 1.67 us
    reshape x1 -> x0, local copies, waits for them, and re-layouts: 1.78 us -> none  [body(): return out.reshape(share, 2, modes)]
    pallas_call x1, Pallas kernels: 49.2 us -> 50.7 us  [body(): pl.pallas_call(functools.partial(kernel, n, chips, chunks, blocks), out_s...]
where the time goes in v2:
time: 52.6 us; the launch traced here: 52.4 us
  Pallas kernels  50.7 us (96%)
  local copies, waits for them, and re-layouts  1.67 us (3%)
    pallas_call x1, Pallas kernels, body(): pl.pallas_call(functools.partial(kernel, n, chips, chunks, blocks), out_s...  50.7 us
    unnamed x1, local copies, waits for them, and re-layouts  1.67 us

profile of v2, /device:TPU:0, one launch (start us, length us, event | category | flops | bytes accessed | tf_op | source)
XLA Modules:
  0.0 52.4 jit_solution(6890951654997479706)
XLA Ops:
  0.0 50.7 %shard_map.37 = f32[512,128]{1,0:T(8,128)} custom-call(s32[8]{0:T(128)} %counts_ref.1, bf16[4096,128]{1,0:T(8,128)(2,1)} %bitcast.2, bf16[2,1024,2048]{2,1,0:T(8,128)(2,1)} %electric_ref.1), custom_call_target="tpu_custom_call" | custom-call | tf_op jit(solution)/shard_map/pallas_call | solution.py:244
  50.7 1.7 %copy.5 = f32[256,2,128]{2,1,0:T(2,128)} copy(f32[256,2,128]{2,1,0:T(2,128)} %bitcast.3) | data formatting | bytes 524288

commit v3 on v2

--- a/solution.py
+++ b/solution.py
@@ -8,7 +8,7 @@
 from jax.sharding import PartitionSpec as P
 
 MESH = pl.DeviceIdType.MESH
-HOP = 2
+HOP = 3
 LAG = 3
 CHUNKS = 4
 BLOCKS = 4
@@ -17,8 +17,8 @@
 def kernel(
     n, chips, chunks, blocks,
     counts_ref, trial_ref, electric_ref, out_ref,
-    wide, vt, ebuf, part, rl, rr, sl, sr, x0, x1, f, r1, g, r2, fin,
-    esem, slsem, rlsem, srsem, rrsem, s1s, s1r, s2s, s2r,
+    held, wide, vt, ebuf, part, rl, rr, sl, sr, x0, x1, f, r1, g, r2, fin,
+    tsem, esem, slsem, rlsem, srsem, rrsem, s1s, s1r, s2s, s2r,
 ):
     cap = ebuf.shape[1]
     points = ebuf.shape[2]
@@ -41,6 +41,8 @@
             esem.at[s, z],
         )
 
+    trial_load = pltpu.make_async_copy(trial_ref, held, tsem)
+    trial_load.start()
     for s in range(blocks):
         load(s, 0).start()
         load(s, 1).start()
@@ -76,7 +78,8 @@
         def _():
             left(k, part).start()
 
-    wide[...] = trial_ref[...].astype(jnp.float32)
+    trial_load.wait()
+    wide[...] = held[...].astype(jnp.float32)
     vt[:modes] = wide[pl.ds(0, points, stride=2), :].astype(jnp.bfloat16).T
     vt[modes:] = wide[pl.ds(1, points, stride=2), :].astype(jnp.bfloat16).T
 
@@ -246,11 +249,12 @@
         out_shape=jax.ShapeDtypeStruct((2 * share, modes), jnp.float32),
         in_specs=[
             pl.BlockSpec(memory_space=pltpu.SMEM),
-            pl.BlockSpec(memory_space=pltpu.VMEM),
+            pl.BlockSpec(memory_space=pl.ANY),
             pl.BlockSpec(memory_space=pl.ANY),
         ],
         out_specs=pl.BlockSpec(memory_space=pltpu.VMEM),
         scratch_shapes=[
+            pltpu.VMEM((2 * points, modes), jnp.bfloat16),
             pltpu.VMEM((2 * points, modes), jnp.float32),
             pltpu.VMEM((2 * modes, points), jnp.bfloat16),
             pltpu.VMEM((2, cap, points), jnp.bfloat16),
@@ -262,7 +266,7 @@
             pltpu.VMEM((chunks, chips, rows, share), jnp.float32),
             pltpu.VMEM((chunks, chips, rows, share), jnp.float32),
             pltpu.VMEM((2 * modes, share), jnp.float32),
-            dma((blocks, 2)),
+            dma(()), dma((blocks, 2)),
             dma((pieces,)), dma((pieces,)), dma((pieces,)), dma((pieces,)),
             dma((chunks, chips)), dma((chunks, chips)),
             dma((chunks, chips)), dma((chunks, chips)),

time: 52.6 us -> 52.8 us (level)
  no operation moved by 1% of the time
where the time goes in v3:
time: 52.8 us; the launch traced here: 52.7 us
  Pallas kernels  51 us (97%)
  local copies, waits for them, and re-layouts  1.67 us (3%)
    pallas_call x1, Pallas kernels, body(): pl.pallas_call(functools.partial(kernel, n, chips, chunks, blocks), out_s...  51 us
    unnamed x1, local copies, waits for them, and re-layouts  1.67 us

profile of v3, /device:TPU:0, one launch (start us, length us, event | category | flops | bytes accessed | tf_op | source)
XLA Modules:
  0.0 52.7 jit_solution(1058328712483480522)
XLA Ops:
  0.0 51.0 %shard_map.37 = f32[512,128]{1,0:T(8,128)} custom-call(s32[8]{0:T(128)} %counts_ref.1, bf16[4096,128]{1,0:T(8,128)(2,1)} %bitcast.2, bf16[2,1024,2048]{2,1,0:T(8,128)(2,1)} %electric_ref.1), custom_call_target="tpu_custom_call" | custom-call | tf_op jit(solution)/shard_map/pallas_call | solution.py:247
  51.0 1.7 %copy.5 = f32[256,2,128]{2,1,0:T(2,128)} copy(f32[256,2,128]{2,1,0:T(2,128)} %bitcast.3) | data formatting | bytes 524288

commit v4 on v2

--- a/solution.py
+++ b/solution.py
@@ -8,7 +8,7 @@
 from jax.sharding import PartitionSpec as P
 
 MESH = pl.DeviceIdType.MESH
-HOP = 2
+HOP = 3
 LAG = 3
 CHUNKS = 4
 BLOCKS = 4

time: 52.6 us -> 51.1 us (0.971)
  Pallas kernels: 50.7 us -> 49.3 us
    pallas_call x1, Pallas kernels: 50.7 us -> 49.3 us  [body(): pl.pallas_call(functools.partial(kernel, n, chips, chunks, blocks), out_s...]
where the time goes in v4:
time: 51.1 us; the launch traced here: 51 us
  Pallas kernels  49.3 us (96%)
  local copies, waits for them, and re-layouts  1.67 us (3%)
    pallas_call x1, Pallas kernels, body(): pl.pallas_call(functools.partial(kernel, n, chips, chunks, blocks), out_s...  49.3 us
    unnamed x1, local copies, waits for them, and re-layouts  1.67 us

profile of v4, /device:TPU:0, one launch (start us, length us, event | category | flops | bytes accessed | tf_op | source)
XLA Modules:
  0.0 51.0 jit_solution(1500062271108712377)
XLA Ops:
  0.0 49.3 %shard_map.37 = f32[512,128]{1,0:T(8,128)} custom-call(s32[8]{0:T(128)} %counts_ref.1, bf16[4096,128]{1,0:T(8,128)(2,1)} %bitcast.2, bf16[2,1024,2048]{2,1,0:T(8,128)(2,1)} %electric_ref.1), custom_call_target="tpu_custom_call" | custom-call | tf_op jit(solution)/shard_map/pallas_call | solution.py:244
  49.3 1.7 %copy.5 = f32[256,2,128]{2,1,0:T(2,128)} copy(f32[256,2,128]{2,1,0:T(2,128)} %bitcast.3) | data formatting | bytes 524288
